TPU v7x, 32 devices: a whole 2x2x4 slice. The times are simulated.
32 devices in a mesh: morton: 8 (over y, x, core), sub: 4 (over z).
Axes of the slice: x: 2, y: 2, z: 4, core: 2. Of those that a mesh axis runs over, the one named last changes fastest.
Arguments:
- leaf_dens: bfloat16 [512, 8, 294], P(('morton', 'sub')), may hold values from -6 to 6
- leaf_sources: int32 [512, 189], P(('morton', 'sub')), may hold values from 0 to 191, as said below
- leaf_classes: int32 [512, 189], P(('morton', 'sub')), may hold values from 0 to 15
- grand_sources: int32 [8, 189], P('morton'), may hold values from 0 to 7
- grand_classes: int32 [8, 189], P('morton'), may hold values from 0 to 15
- up_ops: bfloat16 [8, 294, 294], replicated, may hold values from -0.125 to 0.125
- far_ops: bfloat16 [16, 294, 294], replicated, may hold values from -0.02734375 to 0.02734375
- down_ops: bfloat16 [8, 294, 294], replicated, may hold values from -0.375 to 0.375
Outputs:
- leaf_local: bfloat16 [512, 8, 294], P(('morton', 'sub'))
Inputs may be any that keep to these rules, and one draw needn't show every extreme that they name: `leaf_sources`: positions in the pool of the finest octants of three Morton ranges of 64 octants each (range t // 64 - 1, its own, and the next); rows of the first range never name the range before it and rows of the last never name the range after it.
All inputs are finite; a program needn't handle non-finite values.
Results may differ from a plain program's by a relative error of at most 0.0085.
Values may be sent and summed in bfloat16 or wider, within the bound.
No kernel may reach another device: no remote copies, remote signals or barrier semaphores. Data moves between devices by JAX's collectives and lax.ppermute only.
A program may use at most 64 MiB of HBM per device.

v0:
```python
import jax
import jax.numpy as jnp
from jax import lax
from jax.sharding import PartitionSpec as P


def from_partner(value, axis, distance):
    mask = 2**distance
    pairs = [(source, source ^ mask) for source in range(lax.axis_size(axis))]
    return lax.ppermute(value, axis, pairs)


def padded(cells, sides, width):
    for axis, dim in sides:
        count = lax.axis_size(axis)
        ends = count - 1
        head = lax.slice_in_dim(cells, 0, width, axis=dim)
        tail = lax.slice_in_dim(cells, cells.shape[dim] - width, cells.shape[dim], axis=dim)
        cells = jnp.concatenate(
            [
                lax.ppermute(tail, axis, [(i, (i + 1) % count) for i in range(ends)]),
                cells,
                lax.ppermute(head, axis, [((i + 1) % count, i) for i in range(ends)]),
            ],
            axis=dim,
        )
    return cells


def far_block(pool_rows, sources, classes, far_matrix, rhs_count, width):
    targets = sources.shape[0]
    classes_count = far_matrix.shape[0] // width
    pool_size = pool_rows.shape[0]
    source_hot = (
        sources[:, :, None] == jnp.arange(pool_size, dtype=jnp.int32)[None, None, :]
    ).astype(jnp.bfloat16)
    class_hot = (
        classes[:, :, None] == jnp.arange(classes_count, dtype=jnp.int32)[None, None, :]
    ).astype(jnp.bfloat16)
    counts = jnp.einsum(
        "tec,teq->tcq", class_hot, source_hot, preferred_element_type=jnp.float32
    ).astype(jnp.bfloat16)
    aggregate = jnp.dot(
        counts.reshape(targets * classes_count, pool_size),
        pool_rows,
        preferred_element_type=jnp.float32,
    ).astype(jnp.bfloat16)
    rows_in = aggregate.reshape(targets, classes_count, rhs_count, width).transpose(0, 2, 1, 3)
    rows_in = rows_in.reshape(targets * rhs_count, classes_count * width)
    return jnp.dot(rows_in, far_matrix, preferred_element_type=jnp.float32).reshape(
        targets, rhs_count, width
    )


def shards(
    leaf_dens, leaf_sources, leaf_classes, grand_sources, grand_classes, up_ops, far_ops, down_ops
):
    own_leaves, rhs_count, width = leaf_dens.shape
    classes_count = far_ops.shape[0]
    parents_here = own_leaves // 8
    grand_span = 64 // own_leaves
    sub_index = lax.axis_index("sub")
    position = sub_index % grand_span
    children = leaf_dens.reshape(parents_here, 8, rhs_count, width)
    parent_dens = jnp.einsum(
        "jknw,kwv->jnv", children, up_ops, preferred_element_type=jnp.float32
    ).astype(jnp.bfloat16)
    mine = parent_dens
    for bit_number in range(grand_span.bit_length() - 1):
        partner = from_partner(mine, "sub", bit_number)
        lower_half = sub_index // (1 << bit_number) % 2 == 0
        mine = jnp.where(
            lower_half,
            jnp.concatenate([mine, partner], axis=0),
            jnp.concatenate([partner, mine], axis=0),
        )
    grand_dens = jnp.einsum("knw,kwv->nv", mine, up_ops, preferred_element_type=jnp.float32).astype(
        jnp.bfloat16
    )
    flat_dens = grand_dens.reshape(rhs_count * width)
    piece_len = rhs_count * width // grand_span
    piece = lax.dynamic_slice_in_dim(flat_dens, position * piece_len, piece_len, 0)
    range_pieces = lax.all_gather(piece[None], "sub", axis=0, tiled=True)
    range_dens = range_pieces.reshape(range_pieces.shape[0] // grand_span, rhs_count * width)
    grand_pool = lax.all_gather(range_dens, "morton", axis=0, tiled=True)
    far_matrix = far_ops.reshape(classes_count * width, width)
    row_pick = sub_index // grand_span
    my_sources = lax.dynamic_slice_in_dim(grand_sources, row_pick, 1, 0)[0]
    my_classes = lax.dynamic_slice_in_dim(grand_classes, row_pick, 1, 0)[0]
    grand_count = grand_pool.shape[0]
    source_hot = (my_sources[:, None] == jnp.arange(grand_count, dtype=jnp.int32)[None, :]).astype(
        jnp.bfloat16
    )
    class_hot = (my_classes[:, None] == jnp.arange(classes_count, dtype=jnp.int32)[None, :]).astype(
        jnp.bfloat16
    )
    grand_counts = jnp.dot(class_hot.T, source_hot, preferred_element_type=jnp.float32).astype(
        jnp.bfloat16
    )
    grand_agg = jnp.dot(grand_counts, grand_pool, preferred_element_type=jnp.float32).astype(
        jnp.bfloat16
    )
    grand_rows = grand_agg.reshape(classes_count, rhs_count, width).transpose(1, 0, 2)
    grand_rows = grand_rows.reshape(rhs_count, classes_count * width)
    grand_local = jnp.dot(grand_rows, far_matrix, preferred_element_type=jnp.float32).astype(
        jnp.bfloat16
    )
    parent_ops = lax.dynamic_slice_in_dim(down_ops, position * parents_here, parents_here, 0)
    parent_local = jnp.einsum(
        "nw,jwv->jnv", grand_local, parent_ops, preferred_element_type=jnp.float32
    ).astype(jnp.bfloat16)
    range_leaves = lax.all_gather(leaf_dens, "sub", axis=0, tiled=True)
    leaf_pool = padded(range_leaves, (("morton", 0),), range_leaves.shape[0])
    pool_rows = leaf_pool.reshape(leaf_pool.shape[0], rhs_count * width)
    leaf_far = far_block(pool_rows, leaf_sources, leaf_classes, far_matrix, rhs_count, width)
    downward = jnp.einsum(
        "jnw,kwv->jknv", parent_local, down_ops, preferred_element_type=jnp.float32
    )
    downward = downward.reshape(own_leaves, rhs_count, width)
    return (leaf_far + downward).astype(jnp.bfloat16)


def solution(mesh):
    placed = (
        P(("morton", "sub"), None, None),
        P(("morton", "sub"), None),
        P(("morton", "sub"), None),
        P("morton", None),
        P("morton", None),
        P(),
        P(),
        P(),
    )
    return jax.shard_map(
        shards,
        mesh=mesh,
        in_specs=placed,
        out_specs=P(("morton", "sub"), None, None),
        check_vma=False,
    )
```

profile of v0, /device:TPU:0, one launch (start us, length us, event | category | flops | bytes accessed | tf_op | source)
XLA Modules:
  0.0 82.7 jit_solution(12412377823219016353)
XLA Ops:
  0.0 0.0 copy-start.6
  0.0 0.0 copy-start.5
  0.0 0.0 copy-start
  0.0 0.0 copy-start.2
  0.0 0.0 copy-start.1
  0.0 2.0 %fusion.34 = bf16[2,8,294]{2,1,0:T(8,128)(2,1)S(1)} fusion(bf16[2,8,8,294]{3,2,1,0:T(8,128)(2,1)} %bitcast.77, bf16[8,294,294]{2,0,1:T(8,128)(2,1)} %param.13), kind=kOutput, calls=%fused_computation.25 | convolution fusion | flops 22132320 | bytes 1467648 | tf_op jit(solution)/shard_map/jknw,kwv->jnv/dot_general | solution.py:65
  2.0 3.2 %collective-permute-start.2 = (bf16[2,8,294]{2,1,0:T(8,128)(2,1)S(1)}, bf16[2,8,294]{2,1,0:T(8,128)(2,1)S(1)}, u32[]{:S(2)}, u32[]{:S(2)}) collective-permute-start(bf16[2,8,294]{2,1,0:T(8,128)(2,1)S(1)} %fusion.34), channel_id=1, source_target_pairs={{0,1},{1,0},{2,3},{3,2},{4,5},{5,4},{6,7},{7,6},{8,9},{9,8},{10,11... | collective-permute-start | bytes 28232 | tf_op jit(solution)/shard_map/ppermute | solution.py:10
  5.2 0.0 copy-done
  5.2 14.6 %all_gather.9 = bf16[64,8,294]{2,1,0:T(8,128)(2,1)S(1)} all-gather(bf16[16,8,294]{2,1,0:T(8,128)(2,1)S(1)} %copy-done), channel_id=1, replica_groups=mesh['morton'=8,'sub'=4] {'sub'}, dimensions={0}, use_global_device_ids=true | all-gather | bytes 376320 | tf_op jit(solution)/shard_map/all_gather | solution.py:112
  19.8 1.3 %collective-permute-start = (bf16[64,8,294]{2,1,0:T(8,128)(2,1)S(1)}, bf16[64,8,294]{2,1,0:T(8,128)(2,1)S(1)}, u32[]{:S(2)}, u32[]{:S(2)}) collective-permute-start(bf16[64,8,294]{2,1,0:T(8,128)(2,1)S(1)} %all_gather.9), channel_id=1, source_target_pairs={{0,4},{4,8},{8,12},{12,16},{16,20},{20,24},{24,28},{1,5},{5,9},{9,... | collective-permute-start | bytes 903176 | tf_op jit(solution)/shard_map/ppermute | solution.py:21
  21.1 1.3 %collective-permute-start.1 = (bf16[64,8,294]{2,1,0:T(8,128)(2,1)S(1)}, bf16[64,8,294]{2,1,0:T(8,128)(2,1)S(1)}, u32[]{:S(2)}, u32[]{:S(2)}) collective-permute-start(bf16[64,8,294]{2,1,0:T(8,128)(2,1)S(1)} %all_gather.9), channel_id=1, source_target_pairs={{4,0},{8,4},{12,8},{16,12},{20,16},{24,20},{28,24},{5,1},{9,5},{13... | collective-permute-start | bytes 903176 | tf_op jit(solution)/shard_map/ppermute | solution.py:23
  22.5 0.0 collective-permute-done.2
  22.5 0.8 collective-permute-start.3
  23.2 0.0 copy-done.2
  23.3 0.0 copy-done.1
  23.3 1.5 %fusion.20 = bf16[16,16,192]{2,1,0:T(8,128)(2,1)} fusion(s32[16,189]{1,0:T(8,128)S(1)} %copy-done.1, s32[16,189]{1,0:T(8,128)S(1)} %copy-done.2), kind=kOutput, calls=%fused_computation.20 | convolution fusion | flops 19257600 | bytes 122496 | tf_op jit(solution)/shard_map/tec,teq->tcq/dot_general | solution.py:40
  24.7 0.0 copy-done.6
  24.7 0.6 dynamic-slice
  25.3 0.0 copy-done.5
  25.3 0.6 dynamic-slice.1
  25.9 1.7 %copy.21 = bf16[8,294,294]{2,1,0:T(8,128)(2,1)S(1)} copy(bf16[8,294,294]{2,0,1:T(8,128)(2,1)} %param.15) | data formatting | bytes 2765952 | tf_op args[7]
  27.6 0.0 copy-start.3
  27.7 0.0 copy-start.4
  28.9 0.0 collective-permute-done.3
  28.9 1.9 %fusion.47 = bf16[8,294]{1,0:T(8,128)(2,1)S(1)} fusion(bf16[8,294,294]{2,0,1:T(8,128)(2,1)} %param.13, bf16[4,8,294]{2,1,0:T(8,128)(2,1)S(1)} %collective-permute-done.3, bf16[4,8,294]{2,1,0:T(8,128)(2,1)S(1)} %maximum_select_fusion.2, pred[]{:T(512)S(6)} %eq.80), kind=kOutput, calls=%fused_computation.30 | convolution fusion | flops 11122608 | bytes 1425313 | tf_op jit(solution)/shard_map/knw,kwv->nv/dot_general | solution.py:77
  30.8 0.1 reshape.38
  30.9 0.1 dynamic_slice.9
  31.0 0.2 dynamic-update-slice
  31.2 11.4 %all-reduce = bf16[2352]{0:T(1024)(128)(2,1)S(1)} all-reduce(bf16[2352]{0:T(1024)(128)(2,1)S(1)} %dynamic-update-slice), channel_id=2, replica_groups=mesh['morton'=8,'sub'=4] {'sub'}, use_global_device_ids=true, to_apply=%add | all-reduce | flops 2352 | bytes 9408
  42.6 0.3 dynamic-update-slice.1
  42.9 25.5 %all-reduce.1 = bf16[18816]{0:T(1024)(128)(2,1)S(1)} all-reduce(bf16[18816]{0:T(1024)(128)(2,1)S(1)} %dynamic-update-slice.1), channel_id=3, replica_groups=mesh['morton'=8,'sub'=4] {'morton'}, use_global_device_ids=true, to_apply=%add.1 | all-reduce | flops 18816 | bytes 75264
  68.4 0.1 reshape.44
  68.5 0.0 copy-done.3
  68.5 0.0 copy-done.4
  68.6 0.5 convolution_convert_fusion.1
  69.0 0.2 reshape.40
  69.2 3.0 %fusion.50 = bf16[8,294,1]{1,0,2:T(8,128)(2,1)S(1)} fusion(bf16[16,294,294]{2,0,1:T(8,128)(2,1)} %param.14, bf16[16,8,294]{2,1,0:T(8,128)(2,1)S(1)} %reshape.40), kind=kOutput, calls=%fused_computation.31 | convolution fusion | flops 22129968 | bytes 2845920 | tf_op jit(solution)/shard_map/dot_general | solution.py:105
  72.3 0.6 fusion.6
  72.8 0.0 collective-permute-done
  72.8 0.0 collective-permute-done.1
  72.8 0.2 pad_maximum_fusion
  73.1 0.9 %reshape.35 = bf16[192,2352]{1,0:T(8,128)(2,1)S(1)} reshape(bf16[192,8,294]{2,1,0:T(8,128)(2,1)S(1)} %pad_maximum_fusion) | data formatting | bytes 1806336 | tf_op jit(solution)/shard_map/reshape | solution.py:114
  74.0 1.5 %convolution_convert_fusion = bf16[256,2352]{0,1:T(8,128)(2,1)S(1)} fusion(bf16[256,192]{1,0:T(8,128)(2,1)} %bitcast.79, bf16[192,2352]{1,0:T(8,128)(2,1)S(1)} %reshape.35), kind=kOutput, calls=%fused_computation | convolution fusion | flops 231813120 | bytes 2205696 | tf_op jit(solution)/shard_map/dot_general | solution.py:43
  75.5 0.8 %copy.19 = bf16[256,2352]{1,0:T(8,128)(2,1)S(1)} copy(bf16[256,2352]{0,1:T(8,128)(2,1)S(1)} %convolution_convert_fusion) | data formatting | bytes 2408448 | tf_op jit(solution)/shard_map/convert_element_type | solution.py:47
  76.4 2.0 %reshape.36 = bf16[16,16,8,294]{3,2,1,0:T(8,128)(2,1)S(1)} reshape(bf16[256,2352]{1,0:T(8,128)(2,1)S(1)} %copy.19) | data formatting | bytes 2408448 | tf_op jit(solution)/shard_map/reshape | solution.py:48
  78.3 4.4 %fusion.26 = bf16[16,8,294]{2,1,0:T(8,128)(2,1)} fusion(f32[16,8,294]{2,1,0:T(8,128)S(1)} %bitcast.78, bf16[16,294,294]{2,0,1:T(8,128)(2,1)} %param.14, bf16[16,16,8,294]{3,2,1,0:T(8,128)(2,1)S(1)} %reshape.36), kind=kOutput, calls=%fused_computation.22 | convolution fusion | flops 354117120 | bytes 4195968 | tf_op jit(solution)/shard_map/dot_general | solution.py:50
  (3 shorter events, 0.0 us)
Async XLA Ops:
  0.0 24.7 %copy-start.6 = (u32[32]{0:T(128)S(1)}, u32[32]{0:T(128)}, u32[]{:S(2)}) copy-start(u32[32]{0:T(128)} %constant.71) | copy-start | bytes 388
  0.0 25.3 %copy-start.5 = (u32[32]{0:T(128)S(1)}, u32[32]{0:T(128)}, u32[]{:S(2)}) copy-start(u32[32]{0:T(128)} %constant.76) | copy-start | bytes 388
  0.0 5.2 %copy-start = (bf16[16,8,294]{2,1,0:T(8,128)(2,1)S(1)}, bf16[16,8,294]{2,1,0:T(8,128)(2,1)}, u32[]{:S(2)}) copy-start(bf16[16,8,294]{2,1,0:T(8,128)(2,1)} %param.8) | copy-start | bytes 225796
  0.0 23.2 %copy-start.2 = (s32[16,189]{1,0:T(8,128)S(1)}, s32[16,189]{1,0:T(8,128)}, u32[]{:S(2)}) copy-start(s32[16,189]{1,0:T(8,128)} %param.10) | copy-start | bytes 36292
  0.0 23.2 %copy-start.1 = (s32[16,189]{1,0:T(8,128)S(1)}, s32[16,189]{1,0:T(8,128)}, u32[]{:S(2)}) copy-start(s32[16,189]{1,0:T(8,128)} %param.9) | copy-start | bytes 36292
  2.0 20.4 %collective-permute-start.2 = (bf16[2,8,294]{2,1,0:T(8,128)(2,1)S(1)}, bf16[2,8,294]{2,1,0:T(8,128)(2,1)S(1)}, u32[]{:S(2)}, u32[]{:S(2)}) collective-permute-start(bf16[2,8,294]{2,1,0:T(8,128)(2,1)S(1)} %fusion.34), channel_id=1, source_target_pairs={{0,1},{1,0},{2,3},{3,2},{4,5},{5,4},{6,7},{7,6},{8,9},{9,8},{10,11... | collective-permute-start | bytes 28232 | tf_op jit(solution)/shard_map/ppermute | solution.py:10
  19.8 53.0 %collective-permute-start = (bf16[64,8,294]{2,1,0:T(8,128)(2,1)S(1)}, bf16[64,8,294]{2,1,0:T(8,128)(2,1)S(1)}, u32[]{:S(2)}, u32[]{:S(2)}) collective-permute-start(bf16[64,8,294]{2,1,0:T(8,128)(2,1)S(1)} %all_gather.9), channel_id=1, source_target_pairs={{0,4},{4,8},{8,12},{12,16},{16,20},{20,24},{24,28},{1,5},{5,9},{9,... | collective-permute-start | bytes 903176 | tf_op jit(solution)/shard_map/ppermute | solution.py:21
  21.1 51.7 %collective-permute-start.1 = (bf16[64,8,294]{2,1,0:T(8,128)(2,1)S(1)}, bf16[64,8,294]{2,1,0:T(8,128)(2,1)S(1)}, u32[]{:S(2)}, u32[]{:S(2)}) collective-permute-start(bf16[64,8,294]{2,1,0:T(8,128)(2,1)S(1)} %all_gather.9), channel_id=1, source_target_pairs={{4,0},{8,4},{12,8},{16,12},{20,16},{24,20},{28,24},{5,1},{9,5},{13... | collective-permute-start | bytes 903176 | tf_op jit(solution)/shard_map/ppermute | solution.py:23
  22.5 6.4 %collective-permute-start.3 = (bf16[4,8,294]{2,1,0:T(8,128)(2,1)S(1)}, bf16[4,8,294]{2,1,0:T(8,128)(2,1)S(1)}, u32[]{:S(2)}, u32[]{:S(2)}) collective-permute-start(bf16[4,8,294]{2,1,0:T(8,128)(2,1)S(1)} %maximum_select_fusion.2), channel_id=1, source_target_pairs={{0,2},{1,3},{2,0},{3,1},{4,6},{5,7},{6,4},{7,5},{8,10},{9,11},{10,... | collective-permute-start | bytes 56456 | tf_op jit(solution)/shard_map/ppermute | solution.py:10
  27.6 40.9 %copy-start.3 = (s32[1,189]{1,0:T(1,128)S(1)}, s32[1,189]{1,0:T(1,128)}, u32[]{:S(2)}) copy-start(s32[1,189]{1,0:T(1,128)} %param.11) | copy-start | bytes 2272
  27.7 40.9 %copy-start.4 = (s32[1,189]{1,0:T(1,128)S(1)}, s32[1,189]{1,0:T(1,128)}, u32[]{:S(2)}) copy-start(s32[1,189]{1,0:T(1,128)} %param.12) | copy-start | bytes 2272
where the time goes:
time: 83.1 us; the launch traced here: 82.7 us
  blocking collectives  51.5 us (62%)
  matrix products  15.4 us (19%)
  local copies, waits for them, and re-layouts  7.59 us (9%)
  starting transfers between devices  6.51 us (8%)
  between operations  1.42 us (2%)
    unnamed x2, blocking collectives  36.9 us
    all_gather x1, blocking collectives, shards(): range_leaves = lax.all_gather(leaf_dens, 'sub', axis=0, tiled=True)  14.6 us
    dot_general x1, matrix products, far_block(): jnp.dot(rows_in, far_matrix, preferred_element_type=jnp.float32)  4.39 us
    ppermute x2, starting transfers between devices, from_partner(): return lax.ppermute(value, axis, pairs)  3.91 us
    unnamed x21, local copies, waits for them, and re-layouts  3.43 us
    dot_general x1, matrix products, shards(): jnp.dot(grand_rows, far_matrix, preferred_element_type=jnp.float32)  3.05 us
    dot_general x1, matrix products, shards(): jnp.einsum('jknw,kwv->jnv', children, up_ops, preferred_element_type=jnp....  2.02 us
    reshape x1, local copies, waits for them, and re-layouts, far_block(): aggregate.reshape(targets, classes_count, rhs_count, width)  1.96 us
  transfers between devices with their start and end apart: 4, of which 0 were waited for; matrix products, arithmetic and copies ran while one was open for 14% of the time, Pallas kernels for 0%

commit v1 on v0

--- a/solution.py
+++ b/solution.py
@@ -109,7 +109,9 @@
     parent_local = jnp.einsum(
         "nw,jwv->jnv", grand_local, parent_ops, preferred_element_type=jnp.float32
     ).astype(jnp.bfloat16)
-    range_leaves = lax.all_gather(leaf_dens, "sub", axis=0, tiled=True)
+    range_leaves = jnp.concatenate(
+        lax.all_to_all(jnp.stack([leaf_dens] * lax.axis_size("sub")), "sub", 0, 0), axis=0
+    )
     leaf_pool = padded(range_leaves, (("morton", 0),), range_leaves.shape[0])
     pool_rows = leaf_pool.reshape(leaf_pool.shape[0], rhs_count * width)
     leaf_far = far_block(pool_rows, leaf_sources, leaf_classes, far_matrix, rhs_count, width)

time: 83.1 us -> 78 us (0.939)
  the two profiles are of different devices: /device:TPU:0 before, /device:TPU:6 now
where the time goes in v1:
time: 78 us; the launch traced here: 77.7 us
  blocking collectives  30 us (38%)
  matrix products  15.3 us (20%)
  starting transfers between devices  13 us (17%)
  waiting for transfers between devices  10.7 us (14%)
  local copies, waits for them, and re-layouts  7.15 us (9%)
  between operations  1.49 us (2%)
    unnamed x2, blocking collectives  30 us
    ppermute x1, waiting for transfers between devices, padded(): lax.ppermute(tail, axis, [(i, (i + 1) % count) for i in range(ends)])  5.68 us
    ppermute x2, waiting for transfers between devices, from_partner(): return lax.ppermute(value, axis, pairs)  5.01 us
    ppermute x2, starting transfers between devices, from_partner(): return lax.ppermute(value, axis, pairs)  4.62 us
    dot_general x1, matrix products, far_block(): jnp.dot(rows_in, far_matrix, preferred_element_type=jnp.float32)  4.41 us
    all_to_all x1, starting transfers between devices, shards(): lax.all_to_all(jnp.stack([leaf_dens] * lax.axis_size('sub')), 'sub', 0, 0)  3.86 us
    dot_general x1, matrix products, shards(): jnp.dot(grand_rows, far_matrix, preferred_element_type=jnp.float32)  3.05 us
    ppermute x1, starting transfers between devices, padded(): lax.ppermute(head, axis, [((i + 1) % count, i) for i in range(ends)])  2.59 us
  transfers between devices with their start and end apart: 5, of which 2 were waited for; matrix products, arithmetic and copies ran while one was open for 16% of the time, Pallas kernels for 0%

profile of v1, /device:TPU:6, one launch (start us, length us, event | category | flops | bytes accessed | tf_op | source)
XLA Modules:
  0.0 77.7 jit_solution(5580416774912332954)
XLA Ops:
  0.0 0.0 copy-start
  0.0 2.1 %fusion.35 = bf16[2,8,294]{2,1,0:T(8,128)(2,1)S(1)} fusion(bf16[2,8,8,294]{3,2,1,0:T(8,128)(2,1)} %bitcast.81, bf16[8,294,294]{2,0,1:T(8,128)(2,1)} %param.13), kind=kOutput, calls=%fused_computation.25 | convolution fusion | flops 22132320 | bytes 1467648 | tf_op jit(solution)/shard_map/jknw,kwv->jnv/dot_general | solution.py:65
  2.1 0.0 copy-start.8
  2.1 1.6 %collective-permute-start.2 = (bf16[2,8,294]{2,1,0:T(8,128)(2,1)S(1)}, bf16[2,8,294]{2,1,0:T(8,128)(2,1)S(1)}, u32[]{:S(2)}, u32[]{:S(2)}) collective-permute-start(bf16[2,8,294]{2,1,0:T(8,128)(2,1)S(1)} %fusion.35), channel_id=1, source_target_pairs={{0,1},{1,0},{2,3},{3,2},{4,5},{5,4},{6,7},{7,6},{8,9},{9,8},{10,11... | collective-permute-start | bytes 28232 | tf_op jit(solution)/shard_map/ppermute | solution.py:10
  3.8 0.0 copy-done.1
  3.8 0.8 %stack.2 = bf16[4,16,8,294]{3,2,1,0:T(8,128)(2,1)} broadcast(bf16[16,8,294]{2,1,0:T(8,128)(2,1)S(1)} %copy-done.1), dimensions={1,2,3} | broadcast | bytes 376320 | tf_op jit(solution)/shard_map/stack | solution.py:113
  4.6 3.9 %all-to-all-start = ((bf16[4,16,8,294]{3,2,1,0:T(8,128)(2,1)}), bf16[4,16,8,294]{3,2,1,0:T(8,128)(2,1)S(1)}, u32[]{:S(2)}, u32[]{:S(2)}) async-start(bf16[4,16,8,294]{3,2,1,0:T(8,128)(2,1)} %stack.2), calls=%async_computation | async-start | bytes 786432 | tf_op jit(solution)/shard_map/all_to_all | solution.py:113
  8.4 0.0 copy-done.4
  8.4 0.0 copy-done.3
  8.4 1.5 %fusion.21 = bf16[16,16,192]{2,1,0:T(8,128)(2,1)} fusion(s32[16,189]{1,0:T(8,128)S(1)} %copy-done.3, s32[16,189]{1,0:T(8,128)S(1)} %copy-done.4), kind=kOutput, calls=%fused_computation.20 | convolution fusion | flops 19257600 | bytes 122496 | tf_op jit(solution)/shard_map/tec,teq->tcq/dot_general | solution.py:40
  9.9 0.0 collective-permute-done.2
  10.0 3.0 %collective-permute-start.3 = (bf16[4,8,294]{2,1,0:T(8,128)(2,1)S(1)}, bf16[4,8,294]{2,1,0:T(8,128)(2,1)S(1)}, u32[]{:S(2)}, u32[]{:S(2)}) collective-permute-start(bf16[4,8,294]{2,1,0:T(8,128)(2,1)S(1)} %maximum_select_fusion.2), channel_id=1, source_target_pairs={{0,2},{1,3},{2,0},{3,1},{4,6},{5,7},{6,4},{7,5},{8,10},{9,11},{10,... | collective-permute-start | bytes 56456 | tf_op jit(solution)/shard_map/ppermute | solution.py:10
  12.9 0.0 copy-done
  12.9 0.5 constant_dynamic-slice_fusion
  13.5 0.0 copy-done.9
  13.5 0.6 dynamic-slice.1
  14.1 0.0 copy-done.8
  14.1 0.6 dynamic-slice
  15.9 5.0 %collective-permute-done.3 = bf16[4,8,294]{2,1,0:T(8,128)(2,1)S(1)} collective-permute-done((bf16[4,8,294]{2,1,0:T(8,128)(2,1)S(1)}, bf16[4,8,294]{2,1,0:T(8,128)(2,1)S(1)}, u32[]{:S(2)}, u32[]{:S(2)}) %collective-permute-start.3) | collective-permute-done | bytes 18848 | tf_op jit(solution)/shard_map/ppermute | solution.py:10
  20.9 1.9 %fusion.48 = bf16[8,294]{1,0:T(8,128)(2,1)S(1)} fusion(bf16[8,294,294]{2,0,1:T(8,128)(2,1)} %param.13, bf16[4,8,294]{2,1,0:T(8,128)(2,1)S(1)} %collective-permute-done.3, bf16[4,8,294]{2,1,0:T(8,128)(2,1)S(1)} %maximum_select_fusion.2, pred[]{:T(512)S(6)} %eq.80), kind=kOutput, calls=%fused_computation.30 | convolution fusion | flops 11122608 | bytes 1425313 | tf_op jit(solution)/shard_map/knw,kwv->nv/dot_general | solution.py:77
  22.8 0.1 reshape.45
  22.9 0.1 dynamic_slice.9
  23.0 0.2 dynamic-update-slice
  23.2 9.9 %all-reduce = bf16[2352]{0:T(1024)(128)(2,1)S(1)} all-reduce(bf16[2352]{0:T(1024)(128)(2,1)S(1)} %dynamic-update-slice), channel_id=2, replica_groups=mesh['morton'=8,'sub'=4] {'sub'}, use_global_device_ids=true, to_apply=%add | all-reduce | flops 2352 | bytes 9408
  33.2 0.3 dynamic-update-slice.1
  33.5 20.1 %all-reduce.1 = bf16[18816]{0:T(1024)(128)(2,1)S(1)} all-reduce(bf16[18816]{0:T(1024)(128)(2,1)S(1)} %dynamic-update-slice.1), channel_id=3, replica_groups=mesh['morton'=8,'sub'=4] {'morton'}, use_global_device_ids=true, to_apply=%add.1 | all-reduce | flops 18816 | bytes 75264
  53.6 0.1 reshape.51
  53.7 0.0 copy-done.5
  53.7 0.0 copy-done.6
  53.7 0.4 convolution_convert_fusion.1
  54.1 0.2 reshape.47
  54.3 0.0 all-to-all-done
  54.3 2.6 %collective-permute-start.1 = (bf16[64,8,294]{2,1,0:T(8,128)(2,1)S(1)}, bf16[64,8,294]{2,1,0:T(8,128)(2,1)S(1)}, u32[]{:S(2)}, u32[]{:S(2)}) collective-permute-start(bf16[64,8,294]{2,1,0:T(8,128)(2,1)S(1)} %bitcast.79), channel_id=1, source_target_pairs={{4,0},{8,4},{12,8},{16,12},{20,16},{24,20},{28,24},{5,1},{9,5},{13... | collective-permute-start | bytes 903176 | tf_op jit(solution)/shard_map/ppermute | solution.py:23
  56.9 1.9 %collective-permute-start = (bf16[64,8,294]{2,1,0:T(8,128)(2,1)S(1)}, bf16[64,8,294]{2,1,0:T(8,128)(2,1)S(1)}, u32[]{:S(2)}, u32[]{:S(2)}) collective-permute-start(bf16[64,8,294]{2,1,0:T(8,128)(2,1)S(1)} %bitcast.80), channel_id=1, source_target_pairs={{0,4},{4,8},{8,12},{12,16},{16,20},{20,24},{24,28},{1,5},{5,9},{9,... | collective-permute-start | bytes 903176 | tf_op jit(solution)/shard_map/ppermute | solution.py:21
  58.8 3.0 %fusion.51 = bf16[8,294,1]{1,0,2:T(8,128)(2,1)S(1)} fusion(bf16[16,294,294]{2,0,1:T(8,128)(2,1)} %param.14, bf16[16,8,294]{2,1,0:T(8,128)(2,1)S(1)} %reshape.47), kind=kOutput, calls=%fused_computation.31 | convolution fusion | flops 22129968 | bytes 2845920 | tf_op jit(solution)/shard_map/dot_general | solution.py:105
  61.9 1.3 %fusion.6 = f32[2,8,8,294]{3,1,2,0:T(8,128)} fusion(bf16[8,294,294]{2,0,1:T(8,128)(2,1)S(1)} %copy-done, bf16[8,294,1]{1,0,2:T(8,128)(2,1)S(1)} %fusion.51, bf16[2,294,294]{2,0,1:T(2,128)(2,1)S(1)} %constant_dynamic-slice_fusion), kind=kOutput, calls=%fused_computation.9 | convolution fusion | flops 24898272 | bytes 1883952 | tf_op jit(solution)/shard_map/jnw,kwv->jknv/dot_general | solution.py:118
  63.2 0.3 concatenate.23
  63.5 0.0 collective-permute-done.1
  63.5 0.3 concatenate.24
  63.8 5.7 %collective-permute-done = bf16[64,8,294]{2,1,0:T(8,128)(2,1)S(1)} collective-permute-done((bf16[64,8,294]{2,1,0:T(8,128)(2,1)S(1)}, bf16[64,8,294]{2,1,0:T(8,128)(2,1)S(1)}, u32[]{:S(2)}, u32[]{:S(2)}) %collective-permute-start) | collective-permute-done | bytes 301088 | tf_op jit(solution)/shard_map/ppermute | solution.py:21
  69.4 0.3 concatenate.22
  69.7 0.0 copy-done.7
  69.8 0.6 convolution_convert_fusion
  70.4 0.8 %copy.14 = bf16[256,2352]{1,0:T(8,128)(2,1)S(1)} copy(bf16[256,2352]{0,1:T(8,128)(2,1)S(1)} %convolution_convert_fusion) | data formatting | bytes 2408448 | tf_op jit(solution)/shard_map/convert_element_type | solution.py:47
  71.2 0.0 copy-start.2
  71.3 2.0 %reshape.43 = bf16[16,16,8,294]{3,2,1,0:T(8,128)(2,1)S(1)} reshape(bf16[256,2352]{1,0:T(8,128)(2,1)S(1)} %copy.14) | data formatting | bytes 2408448 | tf_op jit(solution)/shard_map/reshape | solution.py:48
  73.2 0.0 copy-done.2
  73.2 4.4 %fusion.27 = bf16[16,8,294]{2,1,0:T(8,128)(2,1)} fusion(f32[16,8,294]{2,1,0:T(8,128)S(1)} %bitcast.82, bf16[16,294,294]{2,0,1:T(8,128)(2,1)} %param.14, bf16[16,16,8,294]{3,2,1,0:T(8,128)(2,1)S(1)} %reshape.43), kind=kOutput, calls=%fused_computation.22 | convolution fusion | flops 354117120 | bytes 4195968 | tf_op jit(solution)/shard_map/dot_general | solution.py:50
  (10 shorter events, 0.0 us)
Async XLA Ops:
  0.0 3.8 %copy-start.1 = (bf16[16,8,294]{2,1,0:T(8,128)(2,1)S(1)}, bf16[16,8,294]{2,1,0:T(8,128)(2,1)}, u32[]{:S(2)}) copy-start(bf16[16,8,294]{2,1,0:T(8,128)(2,1)} %param.8) | copy-start | bytes 225796
  0.0 8.4 %copy-start.4 = (s32[16,189]{1,0:T(8,128)S(1)}, s32[16,189]{1,0:T(8,128)}, u32[]{:S(2)}) copy-start(s32[16,189]{1,0:T(8,128)} %param.10) | copy-start | bytes 36292
  0.0 8.4 %copy-start.3 = (s32[16,189]{1,0:T(8,128)S(1)}, s32[16,189]{1,0:T(8,128)}, u32[]{:S(2)}) copy-start(s32[16,189]{1,0:T(8,128)} %param.9) | copy-start | bytes 36292
  0.0 12.9 %copy-start = (bf16[8,294,294]{2,0,1:T(8,128)(2,1)S(1)}, bf16[8,294,294]{2,0,1:T(8,128)(2,1)}, u32[]{:S(2)}) copy-start(bf16[8,294,294]{2,0,1:T(8,128)(2,1)} %param.15) | copy-start | bytes 4148932
  2.1 11.3 %copy-start.9 = (u32[32]{0:T(128)S(1)}, u32[32]{0:T(128)}, u32[]{:S(2)}) copy-start(u32[32]{0:T(128)} %constant.76) | copy-start | bytes 388
  2.1 11.9 %copy-start.8 = (u32[32]{0:T(128)S(1)}, u32[32]{0:T(128)}, u32[]{:S(2)}) copy-start(u32[32]{0:T(128)} %constant.71) | copy-start | bytes 388
  2.1 7.8 %collective-permute-start.2 = (bf16[2,8,294]{2,1,0:T(8,128)(2,1)S(1)}, bf16[2,8,294]{2,1,0:T(8,128)(2,1)S(1)}, u32[]{:S(2)}, u32[]{:S(2)}) collective-permute-start(bf16[2,8,294]{2,1,0:T(8,128)(2,1)S(1)} %fusion.35), channel_id=1, source_target_pairs={{0,1},{1,0},{2,3},{3,2},{4,5},{5,4},{6,7},{7,6},{8,9},{9,8},{10,11... | collective-permute-start | bytes 28232 | tf_op jit(solution)/shard_map/ppermute | solution.py:10
  4.6 49.7 %all-to-all-start = ((bf16[4,16,8,294]{3,2,1,0:T(8,128)(2,1)}), bf16[4,16,8,294]{3,2,1,0:T(8,128)(2,1)S(1)}, u32[]{:S(2)}, u32[]{:S(2)}) async-start(bf16[4,16,8,294]{3,2,1,0:T(8,128)(2,1)} %stack.2), calls=%async_computation | async-start | bytes 786432 | tf_op jit(solution)/shard_map/all_to_all | solution.py:113
  9.9 43.7 %copy-start.5 = (s32[1,189]{1,0:T(1,128)S(1)}, s32[1,189]{1,0:T(1,128)}, u32[]{:S(2)}) copy-start(s32[1,189]{1,0:T(1,128)} %param.11) | copy-start | bytes 2272
  9.9 43.7 %copy-start.6 = (s32[1,189]{1,0:T(1,128)S(1)}, s32[1,189]{1,0:T(1,128)}, u32[]{:S(2)}) copy-start(s32[1,189]{1,0:T(1,128)} %param.12) | copy-start | bytes 2272
  10.0 10.9 %collective-permute-start.3 = (bf16[4,8,294]{2,1,0:T(8,128)(2,1)S(1)}, bf16[4,8,294]{2,1,0:T(8,128)(2,1)S(1)}, u32[]{:S(2)}, u32[]{:S(2)}) collective-permute-start(bf16[4,8,294]{2,1,0:T(8,128)(2,1)S(1)} %maximum_select_fusion.2), channel_id=1, source_target_pairs={{0,2},{1,3},{2,0},{3,1},{4,6},{5,7},{6,4},{7,5},{8,10},{9,11},{10,... | collective-permute-start | bytes 56456 | tf_op jit(solution)/shard_map/ppermute | solution.py:10
  54.3 9.2 %collective-permute-start.1 = (bf16[64,8,294]{2,1,0:T(8,128)(2,1)S(1)}, bf16[64,8,294]{2,1,0:T(8,128)(2,1)S(1)}, u32[]{:S(2)}, u32[]{:S(2)}) collective-permute-start(bf16[64,8,294]{2,1,0:T(8,128)(2,1)S(1)} %bitcast.79), channel_id=1, source_target_pairs={{4,0},{8,4},{12,8},{16,12},{20,16},{24,20},{28,24},{5,1},{9,5},{13... | collective-permute-start | bytes 903176 | tf_op jit(solution)/shard_map/ppermute | solution.py:23
  56.9 12.5 %collective-permute-start = (bf16[64,8,294]{2,1,0:T(8,128)(2,1)S(1)}, bf16[64,8,294]{2,1,0:T(8,128)(2,1)S(1)}, u32[]{:S(2)}, u32[]{:S(2)}) collective-permute-start(bf16[64,8,294]{2,1,0:T(8,128)(2,1)S(1)} %bitcast.80), channel_id=1, source_target_pairs={{0,4},{4,8},{8,12},{12,16},{16,20},{20,24},{24,28},{1,5},{5,9},{9,... | collective-permute-start | bytes 903176 | tf_op jit(solution)/shard_map/ppermute | solution.py:21
  63.2 6.6 %copy-start.7 = (bf16[16,16,192]{2,1,0:T(8,128)(2,1)S(1)}, bf16[16,16,192]{2,1,0:T(8,128)(2,1)}, u32[]{:S(2)}) copy-start(bf16[16,16,192]{2,1,0:T(8,128)(2,1)} %fusion.21) | copy-start | bytes 294916
  71.2 2.0 %copy-start.2 = (f32[2,8,8,294]{3,1,2,0:T(8,128)S(1)}, f32[2,8,8,294]{3,1,2,0:T(8,128)}, u32[]{:S(2)}) copy-start(f32[2,8,8,294]{3,1,2,0:T(8,128)} %fusion.6) | copy-start | bytes 451588
